TPU v7x, 256 devices: a whole 4x4x8 slice. The times are simulated.
256 devices in a mesh: pipe: 32 (over z, y), expert: 8 (over x, core).
Axes of the slice: x: 4, y: 4, z: 8, core: 2. Of those that a mesh axis runs over, the one named last changes fastest.
Arguments:
- saved: bfloat16 [2, 1024, 6144], P(None, 'expert', 'pipe'), may hold values from -6 to 6
- top_grad: bfloat16 [2, 1024, 6144], P(None, 'expert', 'pipe'), may hold values from -6 to 6
- norm_gain: float32 [6144], P('pipe'), may hold values from 0.1 to 1.9
- w_gate: bfloat16 [8, 6144, 8192], P('expert', None, 'pipe'), may hold values from -0.078125 to 0.078125
- w_up: bfloat16 [8, 6144, 8192], P('expert', None, 'pipe'), may hold values from -0.078125 to 0.078125
- w_down: bfloat16 [8, 8192, 6144], P('expert', 'pipe'), may hold values from -0.0625 to 0.0625
- routes: int32 [2, 1024, 2], P(None, 'expert'), may hold values from 0 to 7, all different within a row; in each aligned block of 128 rows (0 to 127, 128 to 255, ..., all dimensions but the last counted through in order) at most 48 rows name the same one
- gates: float32 [2, 1024, 2], P(None, 'expert'), may hold values from 0.1 to 0.9
Outputs:
- input_grads: float32 [2, 1024, 6144], P(None, 'expert', 'pipe')
- grad_gain: float32 [6144], P('pipe')
Inputs may be any that keep to these rules, and one draw needn't show every extreme that they name: `routes`: each token names two different experts; in every aligned block of 128 rows of one micro-batch no expert is named more than 48 times, a bound that some block reaches.
All inputs are finite; a program needn't handle non-finite values.
Results may differ from a plain program's by a relative error of at most 0.017.
Values may be sent and summed in bfloat16 or wider, within the bound.
No kernel may reach another device: no remote copies, remote signals or barrier semaphores. Data moves between devices by JAX's collectives and lax.ppermute only.
A program may use at most 128 MiB of HBM per device.

v0:
```python
import jax
import jax.numpy as jnp
from jax import lax
from jax.sharding import Mesh
from jax.sharding import PartitionSpec as P

PIPE = ("pipe_0", "pipe_1")
eps = 1e-05


def from_everyone(x, axis):
    devices = lax.axis_size(axis)
    return lax.all_to_all(jnp.broadcast_to(x[None], (devices, *x.shape)), axis, 0, 0, tiled=True)


def taken_together(x, axis):
    everything = from_everyone(x, axis)
    return jnp.sum(everything, axis=0)


def in_one_piece(arrays, axis, split_dim, concat_dim, along):
    ends, at = ([], 0)
    for a in arrays[:-1]:
        at += a.shape[along]
        ends.append(at)
    both = jnp.concatenate(arrays, axis=along)
    return tuple(
        jnp.split(
            lax.all_to_all(both, axis, split_axis=split_dim, concat_axis=concat_dim, tiled=True),
            ends,
            axis=along,
        )
    )


def rows_first(arrays, axis, dims):
    turned = [jnp.moveaxis(a, dim, 0) for a, dim in zip(arrays, dims)]
    both = jnp.concatenate([t.reshape(len(t), -1) for t in turned], axis=1)
    out, at, gathered = (lax.all_gather(both, axis, axis=0, tiled=True), 0, [])
    for t, dim in zip(turned, dims):
        section = out[:, at : at + t[0].size].reshape(-1, *t.shape[1:])
        gathered.append(jnp.moveaxis(section, 0, dim))
        at += t[0].size
    return tuple(gathered)


def sum_by_axis(terms, axes):
    total = terms.astype(jnp.bfloat16)
    for axis in axes:
        total = lax.psum_scatter(total, axis, scatter_dimension=0, tiled=True)
    return total.astype(jnp.float32)


def slot_matrix(route_block, n_experts, capacity):
    flat = route_block.reshape(-1)
    onehot = (flat[:, None] == jnp.arange(n_experts, dtype=jnp.int32)[None, :]).astype(jnp.int32)
    before = jnp.cumsum(onehot, axis=0) - onehot
    slot = jnp.sum(before * onehot, axis=1)
    target = flat * capacity + slot
    return (target[None, :] == jnp.arange(n_experts * capacity, dtype=jnp.int32)[:, None]).astype(
        jnp.bfloat16
    )


def contract_last(left, right):
    return lax.dot_general(
        left, right, (((1,), (1,)), ((), ())), preferred_element_type=jnp.float32
    )


def body(saved, top_grad, norm_gain, w_gate, w_up, w_down, routes, gates):
    n_pipe = lax.axis_size(PIPE)
    n_experts = lax.axis_size("expert")
    micro, tok, part = saved.shape
    width = part * n_pipe
    capacity = 3 * tok // n_experts
    slots = n_experts * capacity
    wg = w_gate[0]
    wu = w_up[0]
    down_weight = w_down[0]
    hidden_width = wg.shape[1]
    inputs = saved.astype(jnp.float32)
    upstream = top_grad.astype(jnp.float32)
    squares = taken_together(jnp.sum(inputs * inputs, axis=-1), PIPE)
    scale = lax.rsqrt(squares / width + eps)[:, :, None]
    normed = (inputs * scale * norm_gain).astype(jnp.bfloat16)
    placing = jax.vmap(lambda block: slot_matrix(block, n_experts, capacity))(routes)
    pair_grad = (
        (gates[:, :, :, None] * upstream[:, :, None, :])
        .reshape(micro, 2 * tok, part)
        .astype(jnp.bfloat16)
    )
    sent_x = jnp.einsum(
        "msp,mpd->msd", placing, jnp.repeat(normed, 2, axis=1), preferred_element_type=jnp.float32
    ).astype(jnp.bfloat16)
    sent_g = jnp.einsum(
        "msp,mpd->msd", placing, pair_grad, preferred_element_type=jnp.float32
    ).astype(jnp.bfloat16)
    got_x, got_g = in_one_piece((sent_x, sent_g), "expert", 1, 1, 0)
    input_slice, gradient_slice = rows_first((got_x, got_g), PIPE, (2, 2))
    gate_weight_rows = wg
    up_weight_rows = wu
    gate_partial_total = jnp.einsum(
        "wsk,kz->wsz", input_slice, gate_weight_rows, preferred_element_type=jnp.float32
    )
    up_partial_total = jnp.einsum(
        "wsk,kz->wsz", input_slice, up_weight_rows, preferred_element_type=jnp.float32
    )
    hidden_partial_total = jnp.einsum(
        "vun,zn->vuz", gradient_slice, down_weight, preferred_element_type=jnp.float32
    )
    sig = jax.nn.sigmoid(gate_partial_total)
    act = gate_partial_total * sig
    d_a = (
        hidden_partial_total * up_partial_total * sig * (1.0 + gate_partial_total * (1.0 - sig))
    ).astype(jnp.bfloat16)
    d_b = (hidden_partial_total * act).astype(jnp.bfloat16)
    flat_a = d_a.reshape(micro * slots, hidden_width)
    flat_b = d_b.reshape(micro * slots, hidden_width)
    gate_weight_rows = wg
    up_weight_rows = wu
    summed = sum_by_axis(
        contract_last(gate_weight_rows, flat_a) + contract_last(up_weight_rows, flat_b), PIPE
    )
    d_rows = summed.astype(jnp.bfloat16).reshape(part, micro, slots)
    returned = lax.all_to_all(d_rows, "expert", split_axis=2, concat_axis=2, tiled=True)
    d_pairs = jnp.einsum("dms,msp->mpd", returned, placing, preferred_element_type=jnp.float32)
    d_norm = d_pairs.reshape(micro, tok, 2, part).sum(axis=2)
    scaled = norm_gain * d_norm
    inner = taken_together(jnp.sum(scaled * inputs, axis=-1), PIPE)
    d_x = scale * scaled - inputs * scale**3 * (inner / width)[:, :, None]
    input_grads = upstream + d_x
    gain_part = jnp.sum(d_norm * inputs * scale, axis=(0, 1))
    grad_gain = taken_together(gain_part, "expert")
    return (input_grads, grad_gain)


def solution(mesh):
    torus = Mesh(mesh.devices.reshape(8, 4, mesh.shape["expert"]), ("pipe_0", "pipe_1", "expert"))
    in_specs = (
        P(None, "expert", PIPE),
        P(None, "expert", PIPE),
        P(PIPE),
        P("expert", None, PIPE),
        P("expert", None, PIPE),
        P("expert", PIPE, None),
        P(None, "expert", None),
        P(None, "expert", None),
    )
    out_specs = (P(None, "expert", PIPE), P(PIPE))
    return jax.shard_map(body, mesh=torus, in_specs=in_specs, out_specs=out_specs, check_vma=False)
```

profile of v0, /device:TPU:1, one launch (start us, length us, event | category | flops | bytes accessed | tf_op | source)
XLA Modules:
  0.0 480.7 jit_solution(8491837674366570736)
XLA Ops:
  7.2 1.2 copy.84
  9.3 12.2 %all-to-all-start = ((f32[32,2,128]{2,1,0:T(2,128)}), f32[32,2,128]{2,1,0:T(2,128)}, u32[]{:S(2)}, u32[]{:S(2)}) async-start(f32[32,2,128]{2,1,0:T(2,128)} %broadcast_in_dim.8), calls=%async_computation | async-start | bytes 65536 | tf_op jit(solution)/shard_map/all_to_all | solution.py:13
  21.5 0.8 copy.88
  22.6 1.2 reduce-window.6
  24.1 1.0 copy.83
  26.0 0.8 copy.108
  26.8 1.3 fusion.23
  28.1 1.1 convolution_convert_fusion
  29.1 1.0 all-to-all-done
  31.1 0.9 fusion.30
  32.5 1.8 pad_maximum_fusion
  34.3 2.2 copy.94
  36.5 18.5 %all_to_all.26 = bf16[4,384,192]{2,0,1:T(4,128)(2,1)S(1)} all-to-all(bf16[4,384,192]{2,0,1:T(4,128)(2,1)} %copy.94), channel_id=1, replica_groups=mesh['pipe_0'=8,'pipe_1'=4,'expert'=8] {'expert'}, dimensions={1} | all-to-all | bytes 1179648 | tf_op jit(solution)/shard_map/all_to_all | solution.py:29
  55.0 1.4 slice_bitcast_fusion.1
  56.5 2.0 copy.95
  58.5 1.7 copy.115
  60.2 2.0 copy.96
  62.2 1.0 copy.116
  63.1 1.8 pad_maximum_fusion.1
  65.2 147.0 %all-gather.2.cloned.1.call-done = bf16[6144,1536]{1,0:T(8,128)(2,1)} async-done(((bf16[192,1536]{1,0:T(8,128)(2,1)}), bf16[6144,1536]{1,0:T(8,128)(2,1)}) %all-gather.2.cloned.1.call-update) | async-done | bytes 18874384 | tf_op jit(solution)/shard_map/all_gather | solution.py:39
  212.3 14.5 %fusion.42 = (bf16[6144,768]{1,0:T(8,128)(2,1)}, bf16[6144,768]{1,0:T(8,128)(2,1)}) fusion(bf16[6144,1536]{1,0:T(8,128)(2,1)} %all-gather.2.cloned.1.call-done), kind=kLoop, calls=%fused_computation.59 | loop fusion | bytes 37748736 | tf_op jit(solution)/shard_map/slice | solution.py:41
  226.8 12.7 %copy.98 = bf16[6144,768]{0,1:T(8,128)(2,1)} copy(bf16[6144,768]{1,0:T(8,128)(2,1)} %get-tuple-element.12) | data formatting | bytes 18874368 | tf_op jit(solution)/shard_map/slice | solution.py:41
  239.5 12.7 %copy.97 = bf16[6144,768]{0,1:T(8,128)(2,1)} copy(bf16[6144,768]{1,0:T(8,128)(2,1)} %get-tuple-element.13) | data formatting | bytes 18874368 | tf_op jit(solution)/shard_map/slice | solution.py:41
  252.3 5.3 %fusion.1 = f32[2,384,256]{2,1,0:T(8,128)S(1)} fusion(bf16[2,384,6144]{2,1,0:T(8,128)(2,1)} %bitcast.67, bf16[1,6144,256]{2,1,0:T(8,128)(2,1)S(1)} %copy-done), kind=kOutput, calls=%fused_computation.2 | convolution fusion | flops 2415919104 | bytes 13369344 | tf_op jit(solution)/shard_map/wsk,kz->wsz/dot_general | solution.py:103
  257.6 1.1 copy-done.1
  258.7 0.9 copy-done.6
  259.6 3.4 multiply_convert_fusion
  263.4 2.7 fusion.19
  266.1 7.9 %fusion.3 = f32[768,6144]{1,0:T(8,128)} fusion(bf16[768,256]{1,0:T(8,128)(2,1)S(1)} %bitcast.79, bf16[1,6144,256]{2,1,0:T(8,128)(2,1)S(1)} %copy-done), kind=kOutput, calls=%fused_computation.4 | convolution fusion | flops 2415919104 | bytes 22413312 | tf_op jit(solution)/shard_map/dot_general | solution.py:66
  274.0 13.8 %fusion = bf16[6144,768]{0,1:T(8,128)(2,1)} fusion(f32[768,6144]{1,0:T(8,128)} %fusion.3, bf16[768,256]{1,0:T(8,128)(2,1)} %bitcast.77, bf16[1,6144,256]{2,1,0:T(8,128)(2,1)} %param.12), kind=kOutput, calls=%fused_computation.1 | convolution fusion | flops 2425356288 | bytes 31850496 | tf_op jit(solution)/shard_map/dot_general | solution.py:66
  287.9 102.7 %reduce-scatter.5.cloned.1.call-done = bf16[768,768]{0,1:T(8,128)(2,1)} async-done(((bf16[6144,768]{0,1:T(8,128)(2,1)}), bf16[768,768]{0,1:T(8,128)(2,1)}) %reduce-scatter.5.cloned.1.call-update) | async-done | bytes 1179664 | tf_op jit(solution)/shard_map/reduce_scatter | solution.py:50
  390.6 2.4 copy.109
  393.0 24.0 %reduce-scatter.7.cloned.1.call-done = bf16[192,768]{1,0:T(8,128)(2,1)} async-done(((bf16[768,768]{1,0:T(8,128)(2,1)}), bf16[192,768]{1,0:T(8,128)(2,1)}) %reduce-scatter.7.cloned.1.call-update) | async-done | bytes 294928
  417.0 1.9 copy.110
  418.9 1.4 copy.99
  420.3 14.5 %all_to_all.27 = bf16[192,2,384]{0,1,2:T(2,128)(2,1)S(1)} all-to-all(bf16[192,2,384]{0,1,2:T(2,128)(2,1)S(1)} %copy.99), channel_id=1, replica_groups=mesh['pipe_0'=8,'pipe_1'=4,'expert'=8] {'expert'}, dimensions={2} | all-to-all | bytes 589824 | tf_op jit(solution)/shard_map/all_to_all | solution.py:126
  434.8 1.1 fusion.22
  435.9 2.0 copy.101
  437.8 1.4 bitcast_reduce_fusion
  439.3 2.1 fusion.36
  441.9 4.1 all-to-all-start.4
  446.0 1.5 copy.103
  447.5 3.2 all-to-all-done.4
  450.6 1.3 broadcast_in_dim.10
  451.9 8.1 %all-to-all-start.3 = ((f32[32,2,128]{2,1,0:T(2,128)}), f32[32,2,128]{2,1,0:T(2,128)}, u32[]{:S(2)}, u32[]{:S(2)}) async-start(f32[32,2,128]{2,1,0:T(2,128)} %broadcast_in_dim.10), calls=%async_computation.4 | async-start | bytes 65536 | tf_op jit(solution)/shard_map/all_to_all | solution.py:13
  461.4 7.3 %all-to-all-done.3 = f32[32,2,128]{2,1,0:T(2,128)} async-done(((f32[32,2,128]{2,1,0:T(2,128)}), f32[32,2,128]{2,1,0:T(2,128)}, u32[]{:S(2)}, u32[]{:S(2)}) %all-to-all-start.3) | async-done | bytes 32800 | tf_op jit(solution)/shard_map/all_to_all | solution.py:13
  470.2 2.2 fusion.33
  472.4 1.8 copy.107
  (48 shorter events, 8.0 us)
Async XLA Ops:
  7.2 245.1 %copy-start = (bf16[1,6144,256]{2,1,0:T(8,128)(2,1)S(1)}, bf16[1,6144,256]{2,1,0:T(8,128)(2,1)}, u32[]{:S(2)}) copy-start(bf16[1,6144,256]{2,1,0:T(8,128)(2,1)} %param.11) | copy-start | bytes 9437188
  9.3 20.8 %all-to-all-start = ((f32[32,2,128]{2,1,0:T(2,128)}), f32[32,2,128]{2,1,0:T(2,128)}, u32[]{:S(2)}, u32[]{:S(2)}) async-start(f32[32,2,128]{2,1,0:T(2,128)} %broadcast_in_dim.8), calls=%async_computation | async-start | bytes 65536 | tf_op jit(solution)/shard_map/all_to_all | solution.py:13
  21.4 190.8 %all-gather.2.cloned.1.call-start = ((), (), s32[]{:S(2)}) async-start(), calls=%async_computation.7 | async-start | bytes 19464192 | tf_op jit(solution)/shard_map/all_gather | solution.py:39
  25.2 201.6 %copy-start.3 = (bf16[2,128,192]{2,0,1:T(2,128)(2,1)}, bf16[2,128,192]{2,0,1:T(2,128)(2,1)S(1)}, u32[]{:S(2)}) copy-start(bf16[2,128,192]{2,0,1:T(2,128)(2,1)S(1)} %copy.83) | copy-start | bytes 294916
  31.1 195.8 %copy-start.4 = (f32[2,128]{0,1:T(8,128)}, f32[2,128]{0,1:T(8,128)S(1)}, u32[]{:S(2)}) copy-start(f32[2,128]{0,1:T(8,128)S(1)} %copy.87) | copy-start | bytes 3076
  65.0 325.6 %reduce-scatter.5.cloned.1.call-start = ((), (), s32[]{:S(2)}) async-start(), calls=%async_computation.8 | async-start | bytes 10616832 | tf_op jit(solution)/shard_map/reduce_scatter | solution.py:50
  252.2 6.4 %copy-start.1 = (bf16[6144,768]{0,1:T(8,128)(2,1)S(1)}, bf16[6144,768]{0,1:T(8,128)(2,1)}, u32[]{:S(2)}) copy-start(bf16[6144,768]{0,1:T(8,128)(2,1)} %copy.97) | copy-start | bytes 28311556
  252.2 7.3 %copy-start.6 = (bf16[1,256,6144]{2,1,0:T(8,128)(2,1)S(1)}, bf16[1,256,6144]{2,1,0:T(8,128)(2,1)}, u32[]{:S(2)}) copy-start(bf16[1,256,6144]{2,1,0:T(8,128)(2,1)} %param.13) | copy-start | bytes 9437188
  252.2 10.7 %slice-start = ((s8[9437184]{0:T(1024)(128)(4,1)}), s8[4194304]{0:T(1024)(128)(4,1)S(1)}, s32[]{:S(2)}) async-start(s8[9437184]{0:T(1024)(128)(4,1)} %bitcast.68), calls=%async_computation.10 | async-start | bytes 8388608
  252.3 10.7 %slice-start.1 = ((s8[9437184]{0:T(1024)(128)(4,1)}), s8[4194304]{0:T(1024)(128)(4,1)S(1)}, s32[]{:S(2)}) async-start(s8[9437184]{0:T(1024)(128)(4,1)} %bitcast.68), calls=%async_computation.11 | async-start | bytes 8388608
  259.6 3.4 slice-start.2
  259.6 3.8 copy-start.2
  287.8 151.5 %copy-start.5 = (f32[192]{0:T(256)S(1)}, f32[192]{0:T(256)}, u32[]{:S(2)}) copy-start(f32[192]{0:T(256)} %param.10) | copy-start | bytes 2308
  287.8 129.2 %reduce-scatter.7.cloned.1.call-start = ((), (), s32[]{:S(2)}) async-start(), calls=%async_computation.9 | async-start | bytes 1474560
  441.9 8.7 %all-to-all-start.4 = ((f32[8,1,192]{2,1,0:T(1,128)}), f32[8,1,192]{2,1,0:T(1,128)S(1)}, u32[]{:S(2)}, u32[]{:S(2)}) async-start(f32[8,1,192]{2,1,0:T(1,128)} %broadcast_in_dim.11), calls=%async_computation.5 | async-start | bytes 16384 | tf_op jit(solution)/shard_map/all_to_all | solution.py:13
  451.9 16.7 %all-to-all-start.3 = ((f32[32,2,128]{2,1,0:T(2,128)}), f32[32,2,128]{2,1,0:T(2,128)}, u32[]{:S(2)}, u32[]{:S(2)}) async-start(f32[32,2,128]{2,1,0:T(2,128)} %broadcast_in_dim.10), calls=%async_computation.4 | async-start | bytes 65536 | tf_op jit(solution)/shard_map/all_to_all | solution.py:13
Sparse Core Ops, SparseCore 0:
  65.1 147.1 all-gather.1
  288.0 102.5 reduce-scatter.4
  393.1 23.8 reduce-scatter.6
where the time goes:
time: 482 us; the launch traced here: 481 us
  waiting for transfers between devices  285 us (59%)
  local copies, waits for them, and re-layouts  72.2 us (15%)
  matrix products  35.6 us (7%)
  blocking collectives  33 us (7%)
  starting transfers between devices  24.6 us (5%)
  other arithmetic  16 us (3%)
  between operations  13.9 us (3%)
    all_gather x1, waiting for transfers between devices, rows_first(): out, at, gathered = (lax.all_gather(both, axis, axis=0, tiled=True), 0, [])  147 us
    reduce_scatter x1, waiting for transfers between devices, sum_by_axis(): total = lax.psum_scatter(total, axis, scatter_dimension=0, tiled=True)  103 us
    slice x3, local copies, waits for them, and re-layouts, rows_first(): section = out[:, at:at + t[0].size].reshape(-1, *t.shape[1:])  40 us
    all_to_all x3, starting transfers between devices, from_everyone(): lax.all_to_all(jnp.broadcast_to(x[None], (devices, *x.shape)), axis, 0, 0...  24.3 us
    unnamed x4, waiting for transfers between devices  24.1 us
    dot_general x2, matrix products, contract_last(): lax.dot_general(left, right, (((1,), (1,)), ((), ())), preferred_element_...  21.7 us
    all_to_all x1, blocking collectives, in_one_piece(): lax.all_to_all(both, axis, split_axis=split_dim, concat_axis=concat_dim,...  18.5 us
    all_to_all x1, blocking collectives, body(): lax.all_to_all(d_rows, 'expert', split_axis=2, concat_axis=2, tiled=True)  14.5 us
  transfers between devices with their start and end apart: 6, of which 6 were waited for; matrix products, arithmetic and copies ran while one was open for 2% of the time, Pallas kernels for 0%

commit v1 on v0

--- a/solution.py
+++ b/solution.py
@@ -36,7 +36,13 @@
 def rows_first(arrays, axis, dims):
     turned = [jnp.moveaxis(a, dim, 0) for a, dim in zip(arrays, dims)]
     both = jnp.concatenate([t.reshape(len(t), -1) for t in turned], axis=1)
-    out, at, gathered = (lax.all_gather(both, axis, axis=0, tiled=True), 0, [])
+    out, at, gathered = (
+        jnp.concatenate(
+            lax.all_to_all(jnp.stack([both] * lax.axis_size(axis)), axis, 0, 0), axis=0
+        ),
+        0,
+        [],
+    )
     for t, dim in zip(turned, dims):
         section = out[:, at : at + t[0].size].reshape(-1, *t.shape[1:])
         gathered.append(jnp.moveaxis(section, 0, dim))

time: 482 us -> 749 us (1.55)
  blocking collectives: 33 us -> 448 us
  waiting for transfers between devices: 285 us -> 138 us
    all_to_all x0 -> x1, blocking collectives: none -> 415 us  [rows_first(): lax.all_to_all(jnp.stack([both] * lax.axis_size(axis)), axis, 0, 0)]
    all_gather x1 -> x0, waiting for transfers between devices: 147 us -> none  [rows_first(): out, at, gathered = (lax.all_gather(both, axis, axis=0, tiled=True), 0, [])]
    slice x3, local copies, waits for them, and re-layouts: 40 us -> 32 us  [rows_first(): section = out[:, at:at + t[0].size].reshape(-1, *t.shape[1:])]
    unnamed x4 -> x3, waiting for transfers between devices: 24.1 us -> 24.2 us
  transfers between devices with their start and end apart: 6 -> 5, of which waited for: 6 -> 5; matrix products, arithmetic and copies ran while one was open for 2% -> 1% of each run, Pallas kernels for 0% -> 0%
where the time goes in v1:
time: 749 us; the launch traced here: 747 us
  blocking collectives  448 us (60%)
  waiting for transfers between devices  138 us (18%)
  local copies, waits for them, and re-layouts  71.1 us (9%)
  matrix products  35.6 us (5%)
  starting transfers between devices  24.4 us (3%)
  other arithmetic  15.2 us (2%)
  between operations  14.2 us (2%)
    all_to_all x1, blocking collectives, rows_first(): lax.all_to_all(jnp.stack([both] * lax.axis_size(axis)), axis, 0, 0)  415 us
    reduce_scatter x1, waiting for transfers between devices, sum_by_axis(): total = lax.psum_scatter(total, axis, scatter_dimension=0, tiled=True)  103 us
    slice x3, local copies, waits for them, and re-layouts, rows_first(): section = out[:, at:at + t[0].size].reshape(-1, *t.shape[1:])  32 us
    all_to_all x3, starting transfers between devices, from_everyone(): lax.all_to_all(jnp.broadcast_to(x[None], (devices, *x.shape)), axis, 0, 0...  24.4 us
    unnamed x3, waiting for transfers between devices  24.2 us
    dot_general x2, matrix products, contract_last(): lax.dot_general(left, right, (((1,), (1,)), ((), ())), preferred_element_...  21.7 us
    all_to_all x1, blocking collectives, in_one_piece(): lax.all_to_all(both, axis, split_axis=split_dim, concat_axis=concat_dim,...  18.5 us
  transfers between devices with their start and end apart: 5, of which 5 were waited for; matrix products, arithmetic and copies ran while one was open for 1% of the time, Pallas kernels for 0%

profile of v1, /device:TPU:1, one launch (start us, length us, event | category | flops | bytes accessed | tf_op | source)
XLA Modules:
  0.0 746.7 jit_solution(13980217614582786998)
XLA Ops:
  7.2 1.2 copy.84
  9.3 12.2 %all-to-all-start = ((f32[32,2,128]{2,1,0:T(2,128)}), f32[32,2,128]{2,1,0:T(2,128)}, u32[]{:S(2)}, u32[]{:S(2)}) async-start(f32[32,2,128]{2,1,0:T(2,128)} %broadcast_in_dim.8), calls=%async_computation | async-start | bytes 65536 | tf_op jit(solution)/shard_map/all_to_all | solution.py:13
  22.6 1.2 reduce-window.6
  24.1 1.0 copy.83
  26.0 0.8 copy.108
  26.8 1.3 fusion.23
  28.1 1.1 convolution_convert_fusion
  29.1 1.0 all-to-all-done
  31.1 0.9 fusion.30
  32.5 1.8 pad_maximum_fusion
  34.3 2.2 copy.94
  36.5 18.5 %all_to_all.31 = bf16[4,384,192]{2,0,1:T(4,128)(2,1)S(1)} all-to-all(bf16[4,384,192]{2,0,1:T(4,128)(2,1)} %copy.94), channel_id=1, replica_groups=mesh['pipe_0'=8,'pipe_1'=4,'expert'=8] {'expert'}, dimensions={1} | all-to-all | bytes 1179648 | tf_op jit(solution)/shard_map/all_to_all | solution.py:29
  55.0 1.4 slice_bitcast_fusion.1
  56.5 2.0 copy.95
  58.5 1.7 copy.115
  60.2 2.0 copy.96
  62.2 1.0 copy.116
  63.1 1.0 pad_maximum_fusion.1
  64.2 6.7 stack.2
  70.9 415.2 %all_to_all.32 = bf16[32,192,1536]{2,1,0:T(8,128)(2,1)S(1)} all-to-all(bf16[32,192,1536]{2,1,0:T(8,128)(2,1)} %stack.2), channel_id=1, replica_groups=mesh['pipe_0'=8,'pipe_1'=4,'expert'=8] {'pipe_0','pipe_1'}, dimensions={0} | all-to-all | bytes 37748736 | tf_op jit(solution)/shard_map/all_to_all | solution.py:41
  486.0 6.6 fusion.42
  492.6 12.7 %copy.98 = bf16[6144,768]{0,1:T(8,128)(2,1)} copy(bf16[6144,768]{1,0:T(8,128)(2,1)} %get-tuple-element.12) | data formatting | bytes 18874368 | tf_op jit(solution)/shard_map/slice | solution.py:47
  505.3 12.7 %copy.97 = bf16[6144,768]{0,1:T(8,128)(2,1)} copy(bf16[6144,768]{1,0:T(8,128)(2,1)} %get-tuple-element.13) | data formatting | bytes 18874368 | tf_op jit(solution)/shard_map/slice | solution.py:47
  518.0 5.3 fusion.1
  523.4 1.1 copy-done.1
  524.5 0.9 copy-done.6
  525.4 3.4 multiply_convert_fusion
  529.3 2.7 fusion.19
  532.0 7.9 %fusion.3 = f32[768,6144]{1,0:T(8,128)} fusion(bf16[768,256]{1,0:T(8,128)(2,1)S(1)} %bitcast.81, bf16[1,6144,256]{2,1,0:T(8,128)(2,1)S(1)} %copy-done), kind=kOutput, calls=%fused_computation.4 | convolution fusion | flops 2415919104 | bytes 22413312 | tf_op jit(solution)/shard_map/dot_general | solution.py:72
  539.9 13.8 %fusion = bf16[6144,768]{0,1:T(8,128)(2,1)} fusion(f32[768,6144]{1,0:T(8,128)} %fusion.3, bf16[768,256]{1,0:T(8,128)(2,1)} %bitcast.79, bf16[1,6144,256]{2,1,0:T(8,128)(2,1)} %param.12), kind=kOutput, calls=%fused_computation.1 | convolution fusion | flops 2425356288 | bytes 31850496 | tf_op jit(solution)/shard_map/dot_general | solution.py:72
  553.8 102.6 %reduce-scatter.5.cloned.1.call-done = bf16[768,768]{0,1:T(8,128)(2,1)} async-done(((bf16[6144,768]{0,1:T(8,128)(2,1)}), bf16[768,768]{0,1:T(8,128)(2,1)}) %reduce-scatter.5.cloned.1.call-update) | async-done | bytes 1179664 | tf_op jit(solution)/shard_map/reduce_scatter | solution.py:56
  656.3 2.4 copy.109
  658.8 24.1 %reduce-scatter.7.cloned.1.call-done = bf16[192,768]{1,0:T(8,128)(2,1)} async-done(((bf16[768,768]{1,0:T(8,128)(2,1)}), bf16[192,768]{1,0:T(8,128)(2,1)}) %reduce-scatter.7.cloned.1.call-update) | async-done | bytes 294928
  682.9 1.9 copy.110
  684.8 1.4 copy.99
  686.2 14.3 %all_to_all.33 = bf16[192,2,384]{0,1,2:T(2,128)(2,1)S(1)} all-to-all(bf16[192,2,384]{0,1,2:T(2,128)(2,1)S(1)} %copy.99), channel_id=1, replica_groups=mesh['pipe_0'=8,'pipe_1'=4,'expert'=8] {'expert'}, dimensions={2} | all-to-all | bytes 589824 | tf_op jit(solution)/shard_map/all_to_all | solution.py:132
  700.4 1.1 fusion.22
  701.5 2.0 copy.101
  703.5 1.4 bitcast_reduce_fusion
  705.0 2.1 fusion.36
  707.6 4.1 all-to-all-start.5
  711.7 1.5 copy.103
  713.2 3.2 all-to-all-done.5
  716.3 1.3 broadcast_in_dim.10
  717.6 8.2 %all-to-all-start.4 = ((f32[32,2,128]{2,1,0:T(2,128)}), f32[32,2,128]{2,1,0:T(2,128)}, u32[]{:S(2)}, u32[]{:S(2)}) async-start(f32[32,2,128]{2,1,0:T(2,128)} %broadcast_in_dim.10), calls=%async_computation.5 | async-start | bytes 65536 | tf_op jit(solution)/shard_map/all_to_all | solution.py:13
  727.1 7.3 all-to-all-done.4
  736.0 2.2 fusion.33
  738.1 1.8 copy.107
  (47 shorter events, 8.7 us)
Async XLA Ops:
  7.2 510.9 %copy-start = (bf16[1,6144,256]{2,1,0:T(8,128)(2,1)S(1)}, bf16[1,6144,256]{2,1,0:T(8,128)(2,1)}, u32[]{:S(2)}) copy-start(bf16[1,6144,256]{2,1,0:T(8,128)(2,1)} %param.11) | copy-start | bytes 9437188
  9.3 20.8 %all-to-all-start = ((f32[32,2,128]{2,1,0:T(2,128)}), f32[32,2,128]{2,1,0:T(2,128)}, u32[]{:S(2)}, u32[]{:S(2)}) async-start(f32[32,2,128]{2,1,0:T(2,128)} %broadcast_in_dim.8), calls=%async_computation | async-start | bytes 65536 | tf_op jit(solution)/shard_map/all_to_all | solution.py:13
  21.4 634.9 %reduce-scatter.5.cloned.1.call-start = ((), (), s32[]{:S(2)}) async-start(), calls=%async_computation.8 | async-start | bytes 10616832 | tf_op jit(solution)/shard_map/reduce_scatter | solution.py:56
  25.2 45.7 %copy-start.3 = (bf16[2,128,192]{2,0,1:T(2,128)(2,1)}, bf16[2,128,192]{2,0,1:T(2,128)(2,1)S(1)}, u32[]{:S(2)}) copy-start(bf16[2,128,192]{2,0,1:T(2,128)(2,1)S(1)} %copy.83) | copy-start | bytes 294916
  31.1 39.8 %copy-start.4 = (f32[2,128]{0,1:T(8,128)}, f32[2,128]{0,1:T(8,128)S(1)}, u32[]{:S(2)}) copy-start(f32[2,128]{0,1:T(8,128)S(1)} %copy.87) | copy-start | bytes 3076
  518.0 6.4 copy-start.1
  518.0 7.3 copy-start.6
  518.0 10.7 %slice-start = ((s8[9437184]{0:T(1024)(128)(4,1)}), s8[4194304]{0:T(1024)(128)(4,1)S(1)}, s32[]{:S(2)}) async-start(s8[9437184]{0:T(1024)(128)(4,1)} %bitcast.70), calls=%async_computation.10 | async-start | bytes 8388608
  518.0 10.7 %slice-start.1 = ((s8[9437184]{0:T(1024)(128)(4,1)}), s8[4194304]{0:T(1024)(128)(4,1)S(1)}, s32[]{:S(2)}) async-start(s8[9437184]{0:T(1024)(128)(4,1)} %bitcast.70), calls=%async_computation.11 | async-start | bytes 8388608
  525.3 3.4 slice-start.2
  525.4 3.9 copy-start.2
  553.7 151.3 %copy-start.5 = (f32[192]{0:T(256)S(1)}, f32[192]{0:T(256)}, u32[]{:S(2)}) copy-start(f32[192]{0:T(256)} %param.10) | copy-start | bytes 2308
  553.7 129.2 %reduce-scatter.7.cloned.1.call-start = ((), (), s32[]{:S(2)}) async-start(), calls=%async_computation.9 | async-start | bytes 1474560
  707.6 8.7 %all-to-all-start.5 = ((f32[8,1,192]{2,1,0:T(1,128)}), f32[8,1,192]{2,1,0:T(1,128)S(1)}, u32[]{:S(2)}, u32[]{:S(2)}) async-start(f32[8,1,192]{2,1,0:T(1,128)} %broadcast_in_dim.11), calls=%async_computation.6 | async-start | bytes 16384 | tf_op jit(solution)/shard_map/all_to_all | solution.py:13
  717.6 16.8 %all-to-all-start.4 = ((f32[32,2,128]{2,1,0:T(2,128)}), f32[32,2,128]{2,1,0:T(2,128)}, u32[]{:S(2)}, u32[]{:S(2)}) async-start(f32[32,2,128]{2,1,0:T(2,128)} %broadcast_in_dim.10), calls=%async_computation.5 | async-start | bytes 65536 | tf_op jit(solution)/shard_map/all_to_all | solution.py:13
Sparse Core Ops, SparseCore 0:
  553.8 102.4 reduce-scatter.4
  658.9 23.9 reduce-scatter.6
